TPU v7x, 32 devices: a whole 2x2x4 slice. The times are simulated.
32 devices in a mesh: grp: 4 (over y, x), dev: 8 (over z, core).
Axes of the slice: x: 2, y: 2, z: 4, core: 2. Of those that a mesh axis runs over, the one named last changes fastest.
Arguments:
- q_lat: bfloat16 [128, 64, 576], P(('grp', 'dev')), parts along dimension 0, may hold values from -40 to 40
- latent_cache: bfloat16 [128, 256, 576], P(('grp', 'dev')), parts along dimension 0, may hold values from -8 to 8
- lengths: int32 [128], P('grp'), parts along dimension 0, may hold values from 32 to 256, as said below
- moves: int32 [64, 3], P('grp'), parts along dimension 0, may hold values from 0 to 31, as said below
- hidden_in: bfloat16 [128, 3584], P(('grp', 'dev')), parts along dimension 0, may hold values from -6 to 6
- norm_gain: bfloat16 [3584], replicated, may hold values from 0.25 to 1.75
- w_up: bfloat16 [3584, 10240], P(None, 'dev'), may hold values from -0.09375 to 0.09375
- w_down: bfloat16 [10240, 3584], P('dev'), may hold values from -0.0625 to 0.0625
- queue_counts: int32 [32, 8], P(('grp', 'dev')), parts along dimension 0, may hold values from 0 to 63
- deadline: int32 [128], P(('grp', 'dev')), parts along dimension 0, may hold values from 0 to 7
Outputs:
- attn_out: bfloat16 [128, 64, 512], P(('grp', 'dev')), parts along dimension 0
- new_cache: bfloat16 [128, 256, 576], P(('grp', 'dev')), parts along dimension 0
- mixed: bfloat16 [128, 3584], P(('grp', 'dev')), parts along dimension 0
- bucket_load: float32 [32], P('grp'), parts along dimension 0
There are 4 independent parts, one for each index of `grp`. A program takes and returns all parts, laid end to end along the dimension named above; an argument that names none is the same for every part. Nothing has to cross between parts.
Inputs may be any that keep to these rules, and one draw needn't show every extreme that they name: `lengths`: every length is at least 32; some request has exactly 256. `moves`: entry j * 8 + s (j below 2) has source device s and names a request of device s (requests r lie on device r // 4); the requests listed for one device are distinct. In round j every source s sends to (s + k_j) mod 8, with k_j between 1 and 7 the same for all sources of the round and different between rounds; one of the rounds has k_j = 4.
All inputs are finite; a program needn't handle non-finite values.
Results may differ from a plain program's by a relative error of at most 0.002.
The roundings to bfloat16 on the way count: a program that leaves them out, or rounds other values in their place, can miss the bound.
Values may be sent and summed in bfloat16 or wider, within the bound.
A program may use at most 128 MiB of HBM per device.

v0:
```python
from functools import partial
import jax
import jax.numpy as jnp
from jax import lax
from jax.sharding import PartitionSpec as P

VL = 512
MOVE_DEV = 2
BUCKETS = 8
softmax_scale = 192.0 ** (-0.5)


def for_sending(x):

    def short(part):
        return part.astype(jnp.bfloat16) if part.dtype == jnp.float32 else part

    return jax.tree.map(short, x)


def shifted(value, axis, steps):
    count = lax.axis_size(axis)
    pairs = [(source, (source + steps) % count) for source in range(count)]
    return lax.ppermute(value, axis, pairs)


def attend(queries, latent, context_lengths):
    row_count = queries.shape[0]
    head_count = queries.shape[1]
    block_size = min(128, latent.shape[1])
    block_count = (jnp.max(context_lengths) + block_size - 1) // block_size
    initial = (
        jnp.full((row_count, head_count), -1e30, jnp.float32),
        jnp.zeros((row_count, head_count), jnp.float32),
        jnp.zeros((row_count, head_count, VL), jnp.float32),
    )

    def advance(block_index, carried):
        running_max, running_sum, accumulated = carried
        key_block = lax.dynamic_slice_in_dim(latent, block_index * block_size, block_size, 1)
        scores = (
            jnp.einsum("rhc,rkc->rhk", queries, key_block, preferred_element_type=jnp.float32)
            * softmax_scale
        )
        positions = block_index * block_size + jnp.arange(block_size, dtype=jnp.int32)
        included = positions[None, None, :] < context_lengths[:, None, None]
        scores = jnp.where(included, scores, jnp.float32(-1e30))
        new_max = jnp.maximum(running_max, jnp.max(scores, axis=-1))
        factor = jnp.exp(running_max - new_max)
        weights = jnp.where(included, jnp.exp(scores - new_max[:, :, None]), jnp.float32(0.0))
        running_sum = running_sum * factor + jnp.sum(weights, axis=-1)
        product = jnp.einsum(
            "rhk,rkc->rhc",
            weights.astype(jnp.bfloat16),
            key_block[:, :, :VL],
            preferred_element_type=jnp.float32,
        )
        accumulated = accumulated * factor[:, :, None] + product
        return (new_max, running_sum, accumulated)

    final_max, final_sum, accumulated = lax.fori_loop(0, block_count, advance, initial)
    return (accumulated / final_sum[:, :, None]).astype(jnp.bfloat16)


def moved_by(offset, single_row):
    return jax.tree.map(
        lambda part, own: part.astype(own.dtype),
        shifted(for_sending(single_row), "dev", offset),
        single_row,
    )


def send_round(single_row, round_distance, devices):
    branches = [partial(moved_by, offset) for offset in range(1, devices)]
    return lax.switch(round_distance - 1, branches, single_row)


def per_device(
    q_lat, latent_cache, lengths, moves, hidden_in, norm_gain, w_up, w_down, queue_counts, deadline
):
    devices = lax.axis_size("dev")
    my_index = lax.axis_index("dev")
    row_count = latent_cache.shape[0]
    context = latent_cache.shape[1]
    rounds = moves.reshape(MOVE_DEV, devices, 3)
    own_moves = rounds[:, my_index, :]
    leaving = own_moves[:, 0] - my_index * row_count
    distance = (own_moves[:, 2] - my_index) % devices
    own_lengths = lax.dynamic_slice_in_dim(lengths, my_index * row_count, row_count)
    payload = latent_cache[leaving]
    arrivals = []
    for round_index in range(MOVE_DEV):
        arrivals.append(send_round(payload[round_index], distance[round_index], devices))
    travelled = jnp.stack(arrivals, axis=0)
    new_cache = latent_cache.at[leaving].set(travelled[:, :context])
    attn_out = attend(q_lat, latent_cache, own_lengths)
    widened = hidden_in.astype(jnp.float32)
    scaled = lax.rsqrt(jnp.mean(widened * widened, axis=-1, keepdims=True) + 1e-06)
    normed = (widened * scaled * norm_gain.astype(jnp.float32)[None, :]).astype(jnp.bfloat16)
    running = (deadline[:, None] == jnp.arange(BUCKETS, dtype=jnp.int32)[None, :]).astype(
        jnp.float32
    )
    bucket_terms = queue_counts.astype(jnp.float32)[0] + jnp.sum(running, axis=0)
    all_rows = lax.all_gather(normed, "dev", axis=0, tiled=True)
    bucket_load = lax.psum(bucket_terms, "dev")
    hidden_units = jax.nn.silu(jnp.dot(all_rows, w_up, preferred_element_type=jnp.float32)).astype(
        jnp.bfloat16
    )
    partial_sum = lax.psum_scatter(
        jnp.dot(hidden_units, w_down, preferred_element_type=jnp.float32),
        "dev",
        scatter_dimension=0,
        tiled=True,
    )
    mixed = (widened + partial_sum).astype(jnp.bfloat16)
    return (attn_out, new_cache, mixed, bucket_load)


def solution(mesh):
    return jax.shard_map(
        per_device,
        mesh=mesh,
        in_specs=(
            P(("grp", "dev"), None, None),
            P(("grp", "dev"), None, None),
            P("grp"),
            P("grp", None),
            P(("grp", "dev"), None),
            P(),
            P(None, "dev"),
            P("dev", None),
            P(("grp", "dev"), None),
            P(("grp", "dev")),
        ),
        out_specs=(
            P(("grp", "dev"), None, None),
            P(("grp", "dev"), None, None),
            P(("grp", "dev"), None),
            P("grp"),
        ),
        check_vma=False,
    )
```

profile of v0, /device:TPU:0, one launch (start us, length us, event | category | flops | bytes accessed | tf_op | source)
XLA Modules:
  0.0 112.7 jit_solution(7425908061489002161)
XLA Ops:
  7.2 0.6 copy-done.4
  8.2 16.0 %all-gather = bf16[8,4,3584]{2,1,0:T(4,128)(2,1)S(1)} all-gather(bf16[1,4,3584]{2,1,0:T(4,128)(2,1)S(1)} %fusion.19), channel_id=1, replica_groups=mesh['grp'=4,'dev'=8] {'dev'}, dimensions={0}, use_global_device_ids=true | all-gather | bytes 258048 | tf_op jit(solution)/shard_map/all_gather | solution.py:104
  24.2 10.4 %fusion.13 = f32[32,3584]{1,0:T(8,128)} fusion(bf16[1280,3584]{1,0:T(8,128)(2,1)} %param.33, bf16[32,3584]{1,0:T(8,128)(2,1)S(1)} %reshape.87, bf16[3584,1280]{1,0:T(8,128)(2,1)} %param.32), kind=kOutput, calls=%fused_computation.41 | convolution fusion | flops 587407360 | bytes 19038208 | tf_op jit(solution)/shard_map/dot_general | solution.py:110
  34.7 0.7 fusion.23
  36.2 1.0 while.14
  36.3 0.3 fusion.40
  36.7 0.2 fusion.41
  36.9 0.4 convolution_add_fusion.2
  37.7 0.6 fusion.25
  38.3 0.6 gather_fusion
  38.9 0.3 copy.53
  40.5 16.7 %conditional.3 = (bf16[1,256,576]{2,1,0:T(8,128)(2,1)}) conditional(s32[]{:T(128)} %bitcast.31, bf16[2,256,576]{2,1,0:T(8,128)(2,1)S(1)} %copy.53, bf16[2,256,576]{2,1,0:T(8,128)(2,1)S(1)} %copy.53, bf16[2,256,576]{2,1,0:T(8,128)(2,1)S(1)} %copy.53, bf16[2,256,576]{2,1,0:T(8,128)(2,1)S(1)} %copy.53, ...), branch_computations={%region_12.13_spmd, %region_13.14_spmd, %region_14.15_spmd, %regio... | conditional | bytes 1769520 | solution.py:75
  40.6 2.5 %collective-permute-start.9 = (bf16[256,576]{1,0:T(8,128)(2,1)S(1)}, bf16[256,576]{1,0:T(8,128)(2,1)}, u32[]{:S(2)}, u32[]{:S(2)}) collective-permute-start(bf16[256,576]{1,0:T(8,128)(2,1)S(1)} %slice_bitcast_fusion.9), channel_id=1, source_target_pairs={{0,3},{1,4},{2,5},{3,6},{4,7},{5,0},{6,1},{7,2},{8,11},{9,12},{10,... | collective-permute-start | bytes 884744 | tf_op jit(solution)/shard_map/cond/branch_2_fun/ppermute | solution.py:24
  43.1 14.1 %collective-permute-done.9 = bf16[256,576]{1,0:T(8,128)(2,1)} collective-permute-done((bf16[256,576]{1,0:T(8,128)(2,1)S(1)}, bf16[256,576]{1,0:T(8,128)(2,1)}, u32[]{:S(2)}, u32[]{:S(2)}) %collective-permute-start.9) | collective-permute-done | bytes 294944 | tf_op jit(solution)/shard_map/cond/branch_2_fun/ppermute | solution.py:24
  57.2 16.8 %conditional.2 = (bf16[1,256,576]{2,1,0:T(8,128)(2,1)}) conditional(s32[]{:T(128)} %bitcast.30, bf16[2,256,576]{2,1,0:T(8,128)(2,1)S(1)} %copy.53, bf16[2,256,576]{2,1,0:T(8,128)(2,1)S(1)} %copy.53, bf16[2,256,576]{2,1,0:T(8,128)(2,1)S(1)} %copy.53, bf16[2,256,576]{2,1,0:T(8,128)(2,1)S(1)} %copy.53, ...), branch_computations={%region_5.6_spmd, %region_6.7_spmd, %region_7.8_spmd, %region_8.9_... | conditional | bytes 1769520 | solution.py:75
  57.4 16.7 %collective-permute-done.3 = bf16[256,576]{1,0:T(8,128)(2,1)} collective-permute-done((bf16[256,576]{1,0:T(8,128)(2,1)S(1)}, bf16[256,576]{1,0:T(8,128)(2,1)}, u32[]{:S(2)}, u32[]{:S(2)}) %collective-permute-start.3) | collective-permute-done | bytes 294944 | tf_op jit(solution)/shard_map/cond/branch_3_fun/ppermute | solution.py:24
  74.2 1.2 %pad_maximum_fusion = bf16[2,256,576]{2,1,0:T(8,128)(2,1)S(1)} fusion(bf16[1,256,576]{2,1,0:T(8,128)(2,1)} %get-tuple-element.231, bf16[1,256,576]{2,1,0:T(8,128)(2,1)} %get-tuple-element.230), kind=kLoop, calls=%fused_computation.35 | loop fusion | flops 294912 | bytes 1179648 | tf_op jit(solution)/shard_map/stack | solution.py:94
  75.4 0.2 copy.67
  75.6 14.2 %psum.7 = f32[8]{0:T(128)} all-reduce(f32[8]{0:T(128)S(1)} %bitcast_add_fusion), channel_id=1, replica_groups=mesh['grp'=4,'dev'=8] {'dev'}, use_global_device_ids=true, to_apply=%region_23.24 | all-reduce | flops 8 | bytes 64 | tf_op jit(solution)/shard_map/psum | solution.py:105
  89.8 0.8 scatter_fusion
  90.6 0.7 dynamic-slice
  92.0 0.8 divide_convert_fusion
  92.8 11.5 %all-reduce.3.cloned.1.call-done = f32[32,3584]{1,0:T(8,128)} async-done(((f32[32,3584]{1,0:T(8,128)}), f32[32,3584]{1,0:T(8,128)}) %all-reduce.3.cloned.1.call-update) | async-done | bytes 458768
  104.3 1.5 %fusion.18 = bf16[4,3584]{1,0:T(4,128)(2,1)} fusion(bf16[4,3584]{1,0:T(4,128)(2,1)S(1)} %copy-done.3, f32[32,3584]{1,0:T(8,128)} %all-reduce.3.cloned.1.call-done, u32[]{:T(128)S(6)} %multiply.7), kind=kLoop, calls=%fused_computation.46 | loop fusion | flops 43008 | bytes 114692 | tf_op jit(solution)/shard_map/convert_element_type | solution.py:115
  (45 shorter events, 1.3 us)
Async XLA Ops:
  7.2 0.7 copy-start.3
  7.2 0.7 copy-start.4
  7.2 97.2 %all-reduce.3.cloned.1.call-start = ((), (), s32[]{:S(2)}) async-start(), calls=%async_computation | async-start | bytes 917504
  24.2 10.5 %copy-start.6 = (s32[32]{0:T(128)S(1)}, s32[32]{0:T(128)}, u32[]{:S(2)}) copy-start(s32[32]{0:T(128)} %param.28) | copy-start | bytes 388
  24.2 12.0 %copy-start.1 = (bf16[4,256,576]{1,2,0:T(8,128)(2,1)S(1)}, bf16[4,256,576]{1,2,0:T(8,128)(2,1)}, u32[]{:S(2)}) copy-start(bf16[4,256,576]{1,2,0:T(8,128)(2,1)} %param.27) | copy-start | bytes 3538948
  24.2 12.0 %copy-start.2 = (bf16[4,64,576]{2,1,0:T(8,128)(2,1)S(1)}, bf16[4,64,576]{2,1,0:T(8,128)(2,1)}, u32[]{:S(2)}) copy-start(bf16[4,64,576]{2,1,0:T(8,128)(2,1)} %param.26) | copy-start | bytes 884740
  36.2 1.1 copy-start.5
  40.6 16.7 %collective-permute-start.9 = (bf16[256,576]{1,0:T(8,128)(2,1)S(1)}, bf16[256,576]{1,0:T(8,128)(2,1)}, u32[]{:S(2)}, u32[]{:S(2)}) collective-permute-start(bf16[256,576]{1,0:T(8,128)(2,1)S(1)} %slice_bitcast_fusion.9), channel_id=1, source_target_pairs={{0,3},{1,4},{2,5},{3,6},{4,7},{5,0},{6,1},{7,2},{8,11},{9,12},{10,... | collective-permute-start | bytes 884744 | tf_op jit(solution)/shard_map/cond/branch_2_fun/ppermute | solution.py:24
  57.2 16.8 %copy-start.7 = (s32[4]{0:T(128)S(1)}, s32[4]{0:T(128)}, u32[]{:S(2)}) copy-start(s32[4]{0:T(128)} %param.35) | copy-start | bytes 52
  57.3 16.8 %collective-permute-start.3 = (bf16[256,576]{1,0:T(8,128)(2,1)S(1)}, bf16[256,576]{1,0:T(8,128)(2,1)}, u32[]{:S(2)}, u32[]{:S(2)}) collective-permute-start(bf16[256,576]{1,0:T(8,128)(2,1)S(1)} %slice_bitcast_fusion.3), channel_id=1, source_target_pairs={{0,4},{1,5},{2,6},{3,7},{4,0},{5,1},{6,2},{7,3},{8,12},{9,13},{10,... | collective-permute-start | bytes 884744 | tf_op jit(solution)/shard_map/cond/branch_3_fun/ppermute | solution.py:24
  74.1 1.3 %copy-start.8 = (s32[1,8]{1,0:T(1,128)S(1)}, s32[1,8]{1,0:T(1,128)}, u32[]{:S(2)}) copy-start(s32[1,8]{1,0:T(1,128)} %param.34) | copy-start | bytes 100
  75.6 15.0 %copy-start.9 = (u32[32]{0:T(128)S(1)}, u32[32]{0:T(128)}, u32[]{:S(2)}) copy-start(u32[32]{0:T(128)} %constant.94) | copy-start | bytes 388
  90.6 15.3 %copy-start = (bf16[4,256,576]{1,2,0:T(8,128)(2,1)}, bf16[4,256,576]{1,2,0:T(8,128)(2,1)S(1)}, u32[]{:S(2)}) copy-start(bf16[4,256,576]{1,2,0:T(8,128)(2,1)S(1)} %scatter_fusion) | copy-start | bytes 3538948
Sparse Core Ops, SparseCore 0:
  34.8 69.4 all-reduce.2
where the time goes:
time: 113 us
  waiting for transfers between devices  42.4 us (38%)
  blocking collectives  30.2 us (27%)
  between operations  16.9 us (15%)
  matrix products  11.1 us (10%)
  other arithmetic  5.04 us (4%)
  local copies, waits for them, and re-layouts  4.32 us (4%)
  starting transfers between devices  2.65 us (2%)
    ppermute x2, waiting for transfers between devices, shifted(): return lax.ppermute(value, axis, pairs)  30.8 us
    all_gather x1, blocking collectives, per_device(): all_rows = lax.all_gather(normed, 'dev', axis=0, tiled=True)  16 us
    psum x1, blocking collectives, per_device(): bucket_load = lax.psum(bucket_terms, 'dev')  14.2 us
    unnamed x2, waiting for transfers between devices  11.6 us
    dot_general x1, matrix products, per_device(): jnp.dot(hidden_units, w_down, preferred_element_type=jnp.float32)  10.4 us
    ppermute x2, starting transfers between devices, shifted(): return lax.ppermute(value, axis, pairs)  2.61 us
  transfers between devices with their start and end apart: 3, of which 3 were waited for; matrix products, arithmetic and copies ran while one was open for 7% of the time, Pallas kernels for 0%

commit v1 on v0

--- a/solution.py
+++ b/solution.py
@@ -8,6 +8,15 @@
 MOVE_DEV = 2
 BUCKETS = 8
 softmax_scale = 192.0 ** (-0.5)
+
+
+def add_in_pairs(x, axis):
+    size = lax.axis_size(axis)
+    total, stride = (x, 1)
+    while stride < size:
+        total = total + lax.ppermute(total, axis, [(i, i ^ stride) for i in range(size)])
+        stride = 2 * stride
+    return total
 
 
 def for_sending(x):
@@ -102,7 +111,7 @@
     )
     bucket_terms = queue_counts.astype(jnp.float32)[0] + jnp.sum(running, axis=0)
     all_rows = lax.all_gather(normed, "dev", axis=0, tiled=True)
-    bucket_load = lax.psum(bucket_terms, "dev")
+    bucket_load = add_in_pairs(bucket_terms, "dev")
     hidden_units = jax.nn.silu(jnp.dot(all_rows, w_up, preferred_element_type=jnp.float32)).astype(
         jnp.bfloat16
     )

time: 113 us -> 113 us (level)
  blocking collectives: 30.2 us -> 16 us
  waiting for transfers between devices: 42.4 us -> 56 us
    psum x1 -> x0, blocking collectives: 14.2 us -> none  [per_device(): bucket_load = lax.psum(bucket_terms, 'dev')]
    ppermute x0 -> x3, waiting for transfers between devices: none -> 7.9 us  [add_in_pairs(): lax.ppermute(total, axis, [(i, i ^ stride) for i in range(size)])]
    unnamed x2, waiting for transfers between devices: 11.6 us -> 17.4 us
  transfers between devices with their start and end apart: 3 -> 6, of which waited for: 3 -> 5; matrix products, arithmetic and copies ran while one was open for 7% -> 7% of each run, Pallas kernels for 0% -> 0%
where the time goes in v1:
time: 113 us
  waiting for transfers between devices  56 us (50%)
  between operations  16.9 us (15%)
  blocking collectives  16 us (14%)
  matrix products  11.1 us (10%)
  other arithmetic  5.56 us (5%)
  local copies, waits for them, and re-layouts  4.33 us (4%)
  starting transfers between devices  3.01 us (3%)
    ppermute x2, waiting for transfers between devices, shifted(): return lax.ppermute(value, axis, pairs)  30.7 us
    unnamed x2, waiting for transfers between devices  17.4 us
    all_gather x1, blocking collectives, per_device(): all_rows = lax.all_gather(normed, 'dev', axis=0, tiled=True)  16 us
    dot_general x1, matrix products, per_device(): jnp.dot(hidden_units, w_down, preferred_element_type=jnp.float32)  10.4 us
    ppermute x3, waiting for transfers between devices, add_in_pairs(): lax.ppermute(total, axis, [(i, i ^ stride) for i in range(size)])  7.9 us
    ppermute x2, starting transfers between devices, shifted(): return lax.ppermute(value, axis, pairs)  2.43 us
  transfers between devices with their start and end apart: 6, of which 5 were waited for; matrix products, arithmetic and copies ran while one was open for 7% of the time, Pallas kernels for 0%

profile of v1, /device:TPU:0, one launch (start us, length us, event | category | flops | bytes accessed | tf_op | source)
XLA Modules:
  0.0 113.0 jit_solution(5462535165990947602)
XLA Ops:
  7.2 0.6 copy-done.4
  8.2 16.0 %all-gather = bf16[8,4,3584]{2,1,0:T(4,128)(2,1)S(1)} all-gather(bf16[1,4,3584]{2,1,0:T(4,128)(2,1)S(1)} %fusion.19), channel_id=1, replica_groups=mesh['grp'=4,'dev'=8] {'dev'}, dimensions={0}, use_global_device_ids=true | all-gather | bytes 258048 | tf_op jit(solution)/shard_map/all_gather | solution.py:113
  24.2 10.4 %fusion.13 = f32[32,3584]{1,0:T(8,128)} fusion(bf16[1280,3584]{1,0:T(8,128)(2,1)} %param.33, bf16[32,3584]{1,0:T(8,128)(2,1)S(1)} %reshape.87, bf16[3584,1280]{1,0:T(8,128)(2,1)} %param.32), kind=kOutput, calls=%fused_computation.41 | convolution fusion | flops 587407360 | bytes 19038208 | tf_op jit(solution)/shard_map/dot_general | solution.py:119
  34.8 0.4 collective-permute-start.14
  35.2 0.7 fusion.23
  36.7 1.0 while.14
  36.8 0.3 fusion.40
  37.4 0.4 convolution_add_fusion.2
  38.3 0.6 fusion.25
  38.9 0.6 gather_fusion
  41.1 16.6 %conditional.3 = (bf16[1,256,576]{2,1,0:T(8,128)(2,1)}) conditional(s32[]{:T(128)} %bitcast.31, bf16[2,256,576]{2,1,0:T(8,128)(2,1)S(1)} %copy.53, bf16[2,256,576]{2,1,0:T(8,128)(2,1)S(1)} %copy.53, bf16[2,256,576]{2,1,0:T(8,128)(2,1)S(1)} %copy.53, bf16[2,256,576]{2,1,0:T(8,128)(2,1)S(1)} %copy.53, ...), branch_computations={%region_12.13_spmd, %region_13.14_spmd, %region_14.15_spmd, %regio... | conditional | bytes 1769520 | solution.py:84
  41.1 2.4 %collective-permute-start.9 = (bf16[256,576]{1,0:T(8,128)(2,1)S(1)}, bf16[256,576]{1,0:T(8,128)(2,1)}, u32[]{:S(2)}, u32[]{:S(2)}) collective-permute-start(bf16[256,576]{1,0:T(8,128)(2,1)S(1)} %slice_bitcast_fusion.9), channel_id=1, source_target_pairs={{0,3},{1,4},{2,5},{3,6},{4,7},{5,0},{6,1},{7,2},{8,11},{9,12},{10,... | collective-permute-start | bytes 884744 | tf_op jit(solution)/shard_map/cond/branch_2_fun/ppermute | solution.py:33
  43.5 14.1 %collective-permute-done.9 = bf16[256,576]{1,0:T(8,128)(2,1)} collective-permute-done((bf16[256,576]{1,0:T(8,128)(2,1)S(1)}, bf16[256,576]{1,0:T(8,128)(2,1)}, u32[]{:S(2)}, u32[]{:S(2)}) %collective-permute-start.9) | collective-permute-done | bytes 294944 | tf_op jit(solution)/shard_map/cond/branch_2_fun/ppermute | solution.py:33
  57.6 16.7 %conditional.2 = (bf16[1,256,576]{2,1,0:T(8,128)(2,1)}) conditional(s32[]{:T(128)} %bitcast.30, bf16[2,256,576]{2,1,0:T(8,128)(2,1)S(1)} %copy.53, bf16[2,256,576]{2,1,0:T(8,128)(2,1)S(1)} %copy.53, bf16[2,256,576]{2,1,0:T(8,128)(2,1)S(1)} %copy.53, bf16[2,256,576]{2,1,0:T(8,128)(2,1)S(1)} %copy.53, ...), branch_computations={%region_5.6_spmd, %region_6.7_spmd, %region_7.8_spmd, %region_8.9_... | conditional | bytes 1769520 | solution.py:84
  57.7 16.6 %collective-permute-done.3 = bf16[256,576]{1,0:T(8,128)(2,1)} collective-permute-done((bf16[256,576]{1,0:T(8,128)(2,1)S(1)}, bf16[256,576]{1,0:T(8,128)(2,1)}, u32[]{:S(2)}, u32[]{:S(2)}) %collective-permute-start.3) | collective-permute-done | bytes 294944 | tf_op jit(solution)/shard_map/cond/branch_3_fun/ppermute | solution.py:33
  74.3 1.2 %pad_maximum_fusion = bf16[2,256,576]{2,1,0:T(8,128)(2,1)S(1)} fusion(bf16[1,256,576]{2,1,0:T(8,128)(2,1)} %get-tuple-element.231, bf16[1,256,576]{2,1,0:T(8,128)(2,1)} %get-tuple-element.230), kind=kLoop, calls=%fused_computation.35 | loop fusion | flops 294912 | bytes 1179648 | tf_op jit(solution)/shard_map/stack | solution.py:103
  75.8 0.8 scatter_fusion
  76.6 0.7 dynamic-slice
  77.9 0.8 divide_convert_fusion
  78.7 3.6 %collective-permute-done.15 = f32[8]{0:T(128)S(1)} collective-permute-done((f32[8]{0:T(128)S(1)}, f32[8]{0:T(128)S(1)}, u32[]{:S(2)}, u32[]{:S(2)}) %collective-permute-start.15) | collective-permute-done | bytes 64 | tf_op jit(solution)/shard_map/ppermute | solution.py:17
  82.4 4.3 %collective-permute-done.16 = f32[8]{0:T(128)S(1)} collective-permute-done((f32[8]{0:T(128)S(1)}, f32[8]{0:T(128)S(1)}, u32[]{:S(2)}, u32[]{:S(2)}) %collective-permute-start.16) | collective-permute-done | bytes 64 | tf_op jit(solution)/shard_map/ppermute | solution.py:17
  86.8 0.5 add.87
  87.3 17.3 %all-reduce.3.cloned.1.call-done = f32[32,3584]{1,0:T(8,128)} async-done(((f32[32,3584]{1,0:T(8,128)}), f32[32,3584]{1,0:T(8,128)}) %all-reduce.3.cloned.1.call-update) | async-done | bytes 458768
  104.6 1.5 %fusion.18 = bf16[4,3584]{1,0:T(4,128)(2,1)} fusion(bf16[4,3584]{1,0:T(4,128)(2,1)S(1)} %copy-done.3, f32[32,3584]{1,0:T(8,128)} %all-reduce.3.cloned.1.call-done, u32[]{:T(128)S(6)} %multiply.7), kind=kLoop, calls=%fused_computation.46 | loop fusion | flops 43008 | bytes 114692 | tf_op jit(solution)/shard_map/convert_element_type | solution.py:124
  (53 shorter events, 2.1 us)
Async XLA Ops:
  7.2 0.7 copy-start.3
  7.2 0.7 copy-start.4
  7.2 97.4 %all-reduce.3.cloned.1.call-start = ((), (), s32[]{:S(2)}) async-start(), calls=%async_computation | async-start | bytes 917504
  24.2 10.5 %copy-start.7 = (s32[4]{0:T(128)S(1)}, s32[4]{0:T(128)}, u32[]{:S(2)}) copy-start(s32[4]{0:T(128)} %param.35) | copy-start | bytes 52
  24.2 10.6 %copy-start.8 = (s32[1,8]{1,0:T(1,128)S(1)}, s32[1,8]{1,0:T(1,128)}, u32[]{:S(2)}) copy-start(s32[1,8]{1,0:T(1,128)} %param.34) | copy-start | bytes 100
  24.2 11.0 %copy-start.6 = (s32[32]{0:T(128)S(1)}, s32[32]{0:T(128)}, u32[]{:S(2)}) copy-start(s32[32]{0:T(128)} %param.28) | copy-start | bytes 388
  24.2 12.5 %copy-start.1 = (bf16[4,256,576]{1,2,0:T(8,128)(2,1)S(1)}, bf16[4,256,576]{1,2,0:T(8,128)(2,1)}, u32[]{:S(2)}) copy-start(bf16[4,256,576]{1,2,0:T(8,128)(2,1)} %param.27) | copy-start | bytes 3538948
  24.2 12.5 %copy-start.2 = (bf16[4,64,576]{2,1,0:T(8,128)(2,1)S(1)}, bf16[4,64,576]{2,1,0:T(8,128)(2,1)}, u32[]{:S(2)}) copy-start(bf16[4,64,576]{2,1,0:T(8,128)(2,1)} %param.26) | copy-start | bytes 884740
  34.8 43.9 %collective-permute-start.14 = (f32[8]{0:T(128)S(1)}, f32[8]{0:T(128)S(1)}, u32[]{:S(2)}, u32[]{:S(2)}) collective-permute-start(f32[8]{0:T(128)S(1)} %bitcast_add_fusion), channel_id=1, source_target_pairs={{0,1},{1,0},{2,3},{3,2},{4,5},{5,4},{6,7},{7,6},{8,9},{9,8},{10,11... | collective-permute-start | bytes 104 | tf_op jit(solution)/shard_map/ppermute | solution.py:17
  36.7 1.1 copy-start.5
  41.1 16.5 %collective-permute-start.9 = (bf16[256,576]{1,0:T(8,128)(2,1)S(1)}, bf16[256,576]{1,0:T(8,128)(2,1)}, u32[]{:S(2)}, u32[]{:S(2)}) collective-permute-start(bf16[256,576]{1,0:T(8,128)(2,1)S(1)} %slice_bitcast_fusion.9), channel_id=1, source_target_pairs={{0,3},{1,4},{2,5},{3,6},{4,7},{5,0},{6,1},{7,2},{8,11},{9,12},{10,... | collective-permute-start | bytes 884744 | tf_op jit(solution)/shard_map/cond/branch_2_fun/ppermute | solution.py:33
  57.7 16.7 %collective-permute-start.3 = (bf16[256,576]{1,0:T(8,128)(2,1)S(1)}, bf16[256,576]{1,0:T(8,128)(2,1)}, u32[]{:S(2)}, u32[]{:S(2)}) collective-permute-start(bf16[256,576]{1,0:T(8,128)(2,1)S(1)} %slice_bitcast_fusion.3), channel_id=1, source_target_pairs={{0,4},{1,5},{2,6},{3,7},{4,0},{5,1},{6,2},{7,3},{8,12},{9,13},{10,... | collective-permute-start | bytes 884744 | tf_op jit(solution)/shard_map/cond/branch_3_fun/ppermute | solution.py:33
  75.7 0.8 copy-start.9
  76.5 29.6 %copy-start = (bf16[4,256,576]{1,2,0:T(8,128)(2,1)}, bf16[4,256,576]{1,2,0:T(8,128)(2,1)S(1)}, u32[]{:S(2)}) copy-start(bf16[4,256,576]{1,2,0:T(8,128)(2,1)S(1)} %scatter_fusion) | copy-start | bytes 3538948
  78.7 3.6 %collective-permute-start.15 = (f32[8]{0:T(128)S(1)}, f32[8]{0:T(128)S(1)}, u32[]{:S(2)}, u32[]{:S(2)}) collective-permute-start(f32[8]{0:T(128)S(1)} %add.85), channel_id=1, source_target_pairs={{0,2},{1,3},{2,0},{3,1},{4,6},{5,7},{6,4},{7,5},{8,10},{9,11},{10,... | collective-permute-start | bytes 104 | tf_op jit(solution)/shard_map/ppermute | solution.py:17
  82.3 4.5 %collective-permute-start.16 = (f32[8]{0:T(128)S(1)}, f32[8]{0:T(128)S(1)}, u32[]{:S(2)}, u32[]{:S(2)}) collective-permute-start(f32[8]{0:T(128)S(1)} %add.86), channel_id=1, source_target_pairs={{0,4},{1,5},{2,6},{3,7},{4,0},{5,1},{6,2},{7,3},{8,12},{9,13},{10,... | collective-permute-start | bytes 104 | tf_op jit(solution)/shard_map/ppermute | solution.py:17
Sparse Core Ops, SparseCore 0:
  34.8 69.7 all-reduce.2
